TPU v7x, 512 devices: a whole 4x8x8 slice. The times are simulated.
512 devices in a mesh: dp: 32 (over y_lo, z), fsdp: 16 (over x, y_hi, core).
Axes of the slice: x: 4, y: 8 (y_hi: 2, y_lo: 4; y = y_hi * 4 + y_lo), z: 8, core: 2. Of those that a mesh axis runs over, the one named last changes fastest.
Arguments:
- tokens: bfloat16 [65536, 2048], P(('dp', 'fsdp')), may hold values from -6 to 6
- upstream: bfloat16 [65536, 512], P(('dp', 'fsdp')), may hold values from -6 to 6
- value_weight: bfloat16 [2048, 512], P('fsdp'), may hold values from -0.125 to 0.125
- forget_label: int32 [32], P('dp'), may hold values 0 or 1
- copy_index: int32 [32], P('dp'), may hold values from 0 to 1, as said below
- adv_rate: float32 [2], replicated, may hold values from 0.5 to 2
Outputs:
- meta_grad: float32 [2048, 512], P('fsdp')
Inputs may be any that keep to these rules, and one draw needn't show every extreme that they name: `copy_index`: each of the 2 copies is named by exactly 16 sequences.
All inputs are finite; a program needn't handle non-finite values. No bound on the sum of `forget_label` on one device may be relied on, other than what follows from the above.
Results may differ from a plain program's by a relative error of at most 0.0056.
Values may be sent and summed in bfloat16 or wider, within the bound.
A program may use at most 64 MiB of HBM per device.

v0:
```python
import jax
import jax.numpy as jnp
from jax import lax
from jax.sharding import PartitionSpec as P


def first_slope(value):
    sig = jax.nn.sigmoid(value)
    return sig * (1.0 + value * (1.0 - sig))


def second_slope(value):
    sig = jax.nn.sigmoid(value)
    return sig * (1.0 - sig) * (2.0 + value * (1.0 - 2.0 * sig))


def local(tokens, upstream, value_weight, forget_label, copy_index, adv_rate):
    groups = lax.axis_size("fsdp")
    seq_count = lax.axis_size("dp")
    seq_length = tokens.shape[0] * groups
    forget = forget_label[0].astype(jnp.float32)
    onehot = (jnp.arange(adv_rate.shape[0], dtype=jnp.int32) == copy_index[0]).astype(jnp.float32)
    own_rate = jnp.sum(onehot * adv_rate)
    upward = upstream.astype(jnp.float32)

    def project(piece):
        return jnp.dot(tokens, piece, preferred_element_type=jnp.float32)

    primal = project(lax.all_gather(value_weight, "fsdp", axis=0, tiled=True))
    columns = lax.all_to_all(tokens, "fsdp", split_axis=1, concat_axis=0, tiled=True)

    def contract(piece):
        return lax.dot_general(
            columns, piece, (((0,), (0,)), ((), ())), preferred_element_type=jnp.float32
        )

    delta_adv = (forget * upward * first_slope(primal) / seq_length).astype(jnp.bfloat16)
    grad_local = lax.psum_scatter(
        lax.dot_general(
            tokens, delta_adv, (((0,), (0,)), ((), ())), preferred_element_type=jnp.float32
        ),
        "fsdp",
        scatter_dimension=0,
        tiled=True,
    )
    stacked = lax.psum(onehot[:, None, None] * grad_local[None], "dp")
    grad_own = jnp.sum(onehot[:, None, None] * stacked, axis=0)
    attacked = (value_weight.astype(jnp.float32) - own_rate * grad_own).astype(jnp.bfloat16)
    altered = project(lax.all_gather(attacked, "fsdp", axis=0, tiled=True))
    delta_out = ((1.0 - 2.0 * forget) * upward * first_slope(altered) / seq_length).astype(
        jnp.bfloat16
    )
    outer_local = contract(lax.all_gather(delta_out, "fsdp", axis=0, tiled=True))
    outer_all = lax.psum(onehot[:, None, None] * outer_local[None], "dp")
    tangent = jnp.sum(onehot[:, None, None] * outer_all, axis=0).astype(jnp.bfloat16)
    forward_tangent = project(lax.all_gather(tangent, "fsdp", axis=0, tiled=True))
    delta_curv = (forget * upward * second_slope(primal) * forward_tangent / seq_length).astype(
        jnp.bfloat16
    )
    curv_local = contract(lax.all_gather(delta_curv, "fsdp", axis=0, tiled=True))
    curv_sum = lax.psum(own_rate * curv_local, "dp")
    scale = (float(seq_length) / float(seq_count)) ** 0.5
    return scale * (jnp.sum(outer_all, axis=0) - curv_sum)


def solution(mesh):
    in_specs = (
        P(("dp", "fsdp"), None),
        P(("dp", "fsdp"), None),
        P("fsdp", None),
        P("dp"),
        P("dp"),
        P(),
    )
    out_specs = P("fsdp", None)
    return jax.shard_map(local, mesh=mesh, in_specs=in_specs, out_specs=out_specs, check_vma=False)
```

profile of v0, /device:TPU:1, one launch (start us, length us, event | category | flops | bytes accessed | tf_op | source)
XLA Modules:
  0.0 1383.6 jit_solution(12837787341775304741)
XLA Ops:
  8.0 74.9 %all-gather.6.cloned.1.call-done = bf16[2048,512]{1,0:T(8,128)(2,1)} async-done(((bf16[128,512]{1,0:T(8,128)(2,1)}), bf16[2048,512]{1,0:T(8,128)(2,1)}) %all-gather.6.cloned.1.call-update) | async-done | bytes 2097168 | tf_op jit(solution)/shard_map/all_gather | solution.py:29
  82.9 2.2 fusion.21
  85.1 2.7 convolution_bitcast_fusion
  88.6 105.1 %reduce-scatter.2.cloned.1.call-done = f32[128,512]{0,1:T(8,128)} async-done(((f32[2048,512]{0,1:T(8,128)}), f32[128,512]{0,1:T(8,128)}) %reduce-scatter.2.cloned.1.call-update) | async-done | bytes 262160 | tf_op jit(solution)/shard_map/reduce_scatter | solution.py:38
  193.7 1.1 copy.20
  194.8 0.9 broadcast_multiply_fusion.1
  196.5 288.0 %all-reduce.4.cloned.1.call-done = f32[2,128,512]{2,1,0:T(8,128)} async-done(((f32[2,128,512]{2,1,0:T(8,128)}), f32[2,128,512]{2,1,0:T(8,128)}) %all-reduce.4.cloned.1.call-update) | async-done | bytes 524304 | tf_op jit(solution)/shard_map/psum | solution.py:46
  484.5 1.2 multiply_reduce_fusion.1
  485.7 1.3 subtract_convert_fusion
  487.1 84.5 %all-gather.8.cloned.1.call-done = bf16[2048,512]{1,0:T(8,128)(2,1)} async-done(((bf16[128,512]{1,0:T(8,128)(2,1)}), bf16[2048,512]{1,0:T(8,128)(2,1)}) %all-gather.8.cloned.1.call-update) | async-done | bytes 2097168 | tf_op jit(solution)/shard_map/all_gather | solution.py:49
  571.6 2.8 fusion.10
  574.7 17.7 %all_to_all.19 = bf16[128,16,128]{0,2,1:T(8,128)(2,1)S(1)} all-to-all(bf16[128,16,128]{0,2,1:T(8,128)(2,1)S(1)} %bitcast.39), channel_id=1, replica_groups=mesh['dp'=32,'fsdp'=16] {'fsdp'}, dimensions={1} | all-to-all | bytes 1048576 | tf_op jit(solution)/shard_map/all_to_all | solution.py:30
  592.7 51.0 %all-gather.10.cloned.1.call-done = bf16[2048,512]{1,0:T(8,128)(2,1)} async-done(((bf16[128,512]{1,0:T(8,128)(2,1)}), bf16[2048,512]{1,0:T(8,128)(2,1)}) %all-gather.10.cloned.1.call-update) | async-done | bytes 2097168 | tf_op jit(solution)/shard_map/all_gather | solution.py:53
  643.7 2.3 convolution_bitcast_fusion.3
  646.2 0.9 broadcast_multiply_fusion
  647.2 285.2 %all-reduce.6.cloned.1.call-done = f32[2,128,512]{2,1,0:T(8,128)} async-done(((f32[2,128,512]{2,1,0:T(8,128)}), f32[2,128,512]{2,1,0:T(8,128)}) %all-reduce.6.cloned.1.call-update) | async-done | bytes 524304 | tf_op jit(solution)/shard_map/psum | solution.py:54
  932.4 1.9 multiply_reduce_fusion
  934.3 85.3 %all-gather.12.cloned.1.call-done = bf16[2048,512]{1,0:T(8,128)(2,1)} async-done(((bf16[128,512]{1,0:T(8,128)(2,1)}), bf16[2048,512]{1,0:T(8,128)(2,1)}) %all-gather.12.cloned.1.call-update) | async-done | bytes 2097168 | tf_op jit(solution)/shard_map/all_gather | solution.py:56
  1019.6 2.7 fusion.3
  1022.4 64.3 %all-gather.14.cloned.1.call-done = bf16[2048,512]{1,0:T(8,128)(2,1)} async-done(((bf16[128,512]{1,0:T(8,128)(2,1)}), bf16[2048,512]{1,0:T(8,128)(2,1)}) %all-gather.14.cloned.1.call-update) | async-done | bytes 2097168 | tf_op jit(solution)/shard_map/all_gather | solution.py:60
  1086.7 3.7 fusion.2
  1090.6 284.7 %all-reduce.8.cloned.1.call-done = f32[128,512]{0,1:T(8,128)} async-done(((f32[128,512]{0,1:T(8,128)}), f32[128,512]{0,1:T(8,128)}) %all-reduce.8.cloned.1.call-update) | async-done | bytes 262160 | tf_op jit(solution)/shard_map/psum | solution.py:61
  1375.3 1.0 subtract_multiply_fusion.2
  1376.2 0.8 copy.27
  (32 shorter events, 2.7 us)
Async XLA Ops:
  6.5 78.6 %copy-start = (bf16[128,2048]{1,0:T(8,128)(2,1)S(1)}, bf16[128,2048]{1,0:T(8,128)(2,1)}, u32[]{:S(2)}) copy-start(bf16[128,2048]{1,0:T(8,128)(2,1)} %param.6) | copy-start | bytes 1572868
  6.5 78.6 %copy-start.2 = (bf16[128,512]{1,0:T(8,128)(2,1)S(1)}, bf16[128,512]{1,0:T(8,128)(2,1)}, u32[]{:S(2)}) copy-start(bf16[128,512]{1,0:T(8,128)(2,1)} %param.7) | copy-start | bytes 393220
  6.5 76.3 %all-gather.6.cloned.1.call-start = ((), (), s32[]{:S(2)}) async-start(), calls=%async_computation.2 | async-start | bytes 2228224 | tf_op jit(solution)/shard_map/all_gather | solution.py:29
  7.3 186.4 %reduce-scatter.2.cloned.1.call-start = ((), (), s32[]{:S(2)}) async-start(), calls=%async_computation.3 | async-start | bytes 4456448 | tf_op jit(solution)/shard_map/reduce_scatter | solution.py:38
  87.8 108.0 %copy-start.3 = (f32[2]{0:T(128)S(1)}, f32[2]{0:T(128)}, u32[]{:S(2)}) copy-start(f32[2]{0:T(128)} %param.11) | copy-start | bytes 28
  87.8 397.9 %copy-start.1 = (bf16[128,512]{1,0:T(8,128)(2,1)S(1)}, bf16[128,512]{1,0:T(8,128)(2,1)}, u32[]{:S(2)}) copy-start(bf16[128,512]{1,0:T(8,128)(2,1)} %param.8) | copy-start | bytes 393220
  87.9 396.7 %all-reduce.4.cloned.1.call-start = ((), (), s32[]{:S(2)}) async-start(), calls=%async_computation.4 | async-start | bytes 1048576 | tf_op jit(solution)/shard_map/psum | solution.py:46
  195.7 375.9 %all-gather.8.cloned.1.call-start = ((), (), s32[]{:S(2)}) async-start(), calls=%async_computation.5 | async-start | bytes 2228224 | tf_op jit(solution)/shard_map/all_gather | solution.py:49
  487.1 156.6 %all-gather.10.cloned.1.call-start = ((), (), s32[]{:S(2)}) async-start(), calls=%async_computation.6 | async-start | bytes 2228224 | tf_op jit(solution)/shard_map/all_gather | solution.py:53
  574.4 358.0 %all-reduce.6.cloned.1.call-start = ((), (), s32[]{:S(2)}) async-start(), calls=%async_computation.7 | async-start | bytes 1048576 | tf_op jit(solution)/shard_map/psum | solution.py:54
  647.1 372.4 %all-gather.12.cloned.1.call-start = ((), (), s32[]{:S(2)}) async-start(), calls=%async_computation.8 | async-start | bytes 2228224 | tf_op jit(solution)/shard_map/all_gather | solution.py:56
  934.2 152.5 %all-gather.14.cloned.1.call-start = ((), (), s32[]{:S(2)}) async-start(), calls=%async_computation.9 | async-start | bytes 2228224 | tf_op jit(solution)/shard_map/all_gather | solution.py:60
  1022.3 352.9 %all-reduce.8.cloned.1.call-start = ((), (), s32[]{:S(2)}) async-start(), calls=%async_computation.10 | async-start | bytes 524288 | tf_op jit(solution)/shard_map/psum | solution.py:61
Sparse Core Ops, SparseCore 0:
  10.6 72.2 all-gather.5
  88.0 105.6 reduce-scatter.1
  196.6 287.8 all-reduce.3
  487.6 83.9 all-gather.7
  574.7 68.9 all-gather.9
  647.3 285.0 all-reduce.5
  935.6 83.9 all-gather.11
  1022.8 63.8 all-gather.13
  1090.6 284.6 all-reduce.7
where the time goes:
time: 1410 us; the launch traced here: 1380 us
  waiting for transfers between devices  1320 us (94%)
  blocking collectives  17.7 us (1%)
  matrix products  16.4 us (1%)
  between operations  14.6 us (1%)
    psum x1, waiting for transfers between devices, local(): stacked = lax.psum(onehot[:, None, None] * grad_local[None], 'dp')  288 us
    psum x1, waiting for transfers between devices, local(): outer_all = lax.psum(onehot[:, None, None] * outer_local[None], 'dp')  285 us
    psum x1, waiting for transfers between devices, local(): curv_sum = lax.psum(own_rate * curv_local, 'dp')  285 us
    reduce_scatter x1, waiting for transfers between devices, local(): lax.psum_scatter(lax.dot_general(tokens, delta_adv, (((0,), (0,)), ((), (...  105 us
    all_gather x1, waiting for transfers between devices, local(): lax.all_gather(tangent, 'fsdp', axis=0, tiled=True)  85.3 us
    all_gather x1, waiting for transfers between devices, local(): altered = project(lax.all_gather(attacked, 'fsdp', axis=0, tiled=True))  84.5 us
    all_gather x1, waiting for transfers between devices, local(): primal = project(lax.all_gather(value_weight, 'fsdp', axis=0, tiled=True))  74.9 us
    all_gather x1, waiting for transfers between devices, local(): lax.all_gather(delta_curv, 'fsdp', axis=0, tiled=True)  64.3 us
  transfers between devices with their start and end apart: 9, of which 9 were waited for; matrix products, arithmetic and copies ran while one was open for 0% of the time, Pallas kernels for 0%

commit v1 on v0

v1 whole, which is shorter than its diff:
```python
import jax
import jax.numpy as jnp
from jax import lax
from jax.experimental import pallas as pl
from jax.experimental.pallas import tpu as pltpu
from jax.sharding import PartitionSpec as P

F32, BF16 = jnp.float32, jnp.bfloat16
NX, NYL, N = 4, 4, 8
TOK, DW, E, B, CH = 128, 2048, 512, 64, 128
LEN = 2048.0
SCALE = 8.0


def first_slope(value):
    sig = jax.nn.sigmoid(value)
    return sig * (1.0 + value * (1.0 - sig))


def second_slope(value):
    sig = jax.nn.sigmoid(value)
    return sig * (1.0 - sig) * (2.0 + value * (1.0 - 2.0 * sig))


W_, R_, C_ = 0, 1, 2


def rs1_(s, k):
    return 4 + 2 * s + k


def rs2_(s, k):
    return 10 + 2 * s + k


def ag2_(s, k):
    return 16 + 2 * s + k


def ag1_(s, k):
    return 20 + 2 * s + k


F1_, F2_, F3_, X_, GROUPS = 24, 26, 28, 29, 46


def chunk_of(k, p):
    return (p % 4) * 4 + (p // 4) * 2 + k


def kernel(
    tok_ref, up_ref, w_ref, forget_ref, copy_ref, rate_ref, out_ref,
    xbuf, wsrc, wrecv, rsrc, rrecv, crecv, wt, wown, prim, curv, delta,
    s1, r1, s2, r2, s2c, r2c, a2s, a2r, a1s, a1r, osum, tile, f1r, f2r, f3r,
    ssem, rsem, lsem,
):
    dp, fs = lax.axis_index("dp"), lax.axis_index("fsdp")
    yl, z = dp // 8, dp % 8
    x, yh, c = fs // 4, (fs // 2) % 2, fs % 2
    y = yh * 4 + yl
    place = (y, z)

    def ring_device(ring, p):
        if ring == 0:
            return ((p % 4) * 8 + z, x * 4 + (p // 4) * 2 + c)
        return (yl * 8 + p, fs)

    def group_device(dx, dc):
        return (dp, ((x + dx) % NX) * 4 + yh * 2 + (c + dc) % 2)

    def mirror_device(dx, dc):
        return ((3 - yl) * 8 + z, ((x + dx) % NX) * 4 + (1 - yh) * 2 + (c + dc) % 2)

    def send(src, dst, out_group, in_group, device):
        pltpu.make_async_remote_copy(
            src_ref=src, dst_ref=dst, send_sem=ssem.at[out_group], recv_sem=rsem.at[in_group],
            device_id=device, device_id_type=pl.DeviceIdType.MESH,
        ).start()

    def arrived(ref, group):
        pltpu.make_async_copy(ref, ref, rsem.at[group]).wait()

    def gone(ref, group):
        pltpu.make_async_copy(ref, ref, ssem.at[group]).wait()

    def spread(ring, group, source, dst):
        me = place[ring]

        def step(o, carry):
            p = (me + o) % N
            send(source(p), dst.at[me], group, group, ring_device(ring, p))
            return carry

        lax.fori_loop(1, N, step, 0)

    own = pltpu.make_async_copy(tok_ref, xbuf.at[pl.ds(0, TOK)], lsem)
    own.start()
    barrier = pltpu.get_barrier_semaphore()
    for dx in range(NX):
        for dc in range(2):
            if dx or dc:
                pl.semaphore_signal(barrier, inc=1, device_id=group_device(dx, dc), device_id_type=pl.DeviceIdType.MESH)
            pl.semaphore_signal(barrier, inc=1, device_id=mirror_device(dx, dc), device_id_type=pl.DeviceIdType.MESH)
    for ring in range(2):

        def greet(o, carry, ring=ring):
            device = ring_device(ring, (place[ring] + o) % N)
            pl.semaphore_signal(barrier, inc=1, device_id=device, device_id_type=pl.DeviceIdType.MESH)
            return carry

        lax.fori_loop(1, N, greet, 0)

    wsrc[...] = w_ref[...].T.reshape(8, B, CH)
    rsrc[...] = up_ref[...].T.reshape(8, B, TOK)
    copy = copy_ref[0].astype(F32)
    forget = forget_ref[0].astype(F32)
    rate0, rate1 = rate_ref[0], rate_ref[1]
    own_rate = rate0 * (1.0 - copy) + rate1 * copy
    crecv[0, y] = jnp.full((8, 128), copy, F32)
    crecv[1, z] = jnp.full((8, 128), copy, F32)
    own.wait()
    pl.semaphore_wait(barrier, 29)

    block = 2 * x + c
    for dx in range(NX):
        for dc in range(2):
            to = 2 * ((x + dx) % NX) + (c + dc) % 2
            if dx or dc:
                send(wsrc.at[to], wrecv.at[fs], W_, W_, group_device(dx, dc))
            send(wsrc.at[to], wrecv.at[fs], W_, W_, mirror_device(dx, dc))
    wrecv[fs] = wsrc[block]
    for dx in range(NX):
        for dc in range(2):
            if dx or dc:
                to = 2 * ((x + dx) % NX) + (c + dc) % 2
                send(rsrc.at[to], rrecv.at[2 * (-dx % NX) + dc], R_, R_, group_device(dx, dc))
    rrecv[0] = rsrc[block]

    def part(slot, half):
        return xbuf.at[pl.ds(slot * TOK + half * (TOK // 2), TOK // 2)]

    def send_part(from_slot, to_slot, half, dx, dc):
        send(part(from_slot, half), part(to_slot, half), X_, X_ + 1 + 2 * to_slot + half, group_device(dx, dc))

    def part_arrived(slot, half):
        arrived(part(slot, half), X_ + 1 + 2 * slot + half)

    send_part(0, 6, 0, 1, 0)
    send_part(0, 2, 1, 3, 0)
    send_part(0, 6, 1, 1, 0)
    send_part(0, 2, 0, 3, 0)
    send_part(0, 1, 0, 0, 1)
    send_part(0, 1, 1, 0, 1)
    for ring in range(2):
        spread(ring, C_ + ring, lambda p, ring=ring: crecv.at[ring, place[ring]], crecv.at[ring])

    arrived(wrecv.at[pl.ds(0, 15)], W_)
    for f in range(16):
        wt[:, f * CH:(f + 1) * CH] = wrecv[f]
    for k in range(2):
        wown[k] = wrecv[chunk_of(k, place[k])].astype(F32).reshape(8, 8, CH)
    arrived(rrecv.at[pl.ds(0, 7)], R_)

    def first_pass(slot):
        rows = slice(slot * TOK, (slot + 1) * TOK)
        value = lax.dot_general(wt[...], xbuf[rows, :], (((1,), (1,)), ((), ())), preferred_element_type=F32)
        prim[:, rows] = value
        delta[:, rows] = (forget * rrecv[slot].astype(F32) * first_slope(value) / LEN).astype(BF16)

    first_pass(0)
    part_arrived(6, 0)
    send_part(6, 4, 0, 1, 0)
    send_part(6, 7, 0, 0, 1)
    part_arrived(2, 1)
    send_part(2, 4, 1, 3, 0)
    send_part(2, 3, 1, 0, 1)
    part_arrived(1, 0)
    part_arrived(1, 1)
    first_pass(1)
    part_arrived(6, 1)
    send_part(6, 7, 1, 0, 1)
    part_arrived(2, 0)
    send_part(2, 3, 0, 0, 1)
    first_pass(6)
    first_pass(2)
    for slot in (7, 3):
        part_arrived(slot, 0)
        part_arrived(slot, 1)
        first_pass(slot)
    for half in range(2):
        part_arrived(4, half)
        send_part(4, 5, half, 0, 1)
    first_pass(4)
    part_arrived(5, 0)
    part_arrived(5, 1)
    first_pass(5)

    def reduce_first(s, factor=None):
        left = delta[...]

        def start(o):
            for k in range(2):
                p = (place[k] + o) % N
                send(s1.at[s, k, p], r1.at[s, k, place[k]], rs1_(s, k), rs1_(s, k), ring_device(k, p))

        def step(i, carry):
            o = i + 1
            spots = [(place[k] + o) % N for k in range(2)]
            right = jnp.concatenate(
                [xbuf[:, pl.ds(pl.multiple_of(chunk_of(k, spots[k]) * CH, CH), CH)] for k in range(2)], axis=1)
            sums = jnp.dot(left, right, preferred_element_type=F32)
            if factor is not None:
                sums = factor * sums
            for k in range(2):
                s1[s, k, spots[k]] = sums[:, k * CH:(k + 1) * CH].astype(BF16)
            pl.when(i > 0)(lambda: start(i))
            return carry

        lax.fori_loop(0, N, step, 0)

    def own_first(s, k):
        r1[s, k, place[k]] = s1[s, k, place[k]]

    def reduce_second(s, k):
        arrived(r1.at[s, k, pl.ds(0, 7)], rs1_(s, k))
        own_first(s, k)
        ring = 1 - k
        sums = [jnp.zeros((B, CH), F32) for _ in range(2)]
        for p in range(N):
            piece = r1[s, k, p].astype(F32)
            mark = crecv[k, p, 0:1, :]
            sums[0] = sums[0] + piece * (1.0 - mark)
            sums[1] = sums[1] + piece * mark
        for copy_at in range(2):
            s2[s, k, :, copy_at] = sums[copy_at].reshape(8, 8, CH)
        spread(ring, rs2_(s, k), lambda p: s2.at[s, k, p], r2.at[s, k])

    def owned(s, k):
        me = place[1 - k]
        r2[s, k, me] = s2[s, k, me]
        arrived(r2.at[s, k, pl.ds(0, 7)], rs2_(s, k))
        total = r2[s, k, 0]
        for p in range(1, N):
            total = total + r2[s, k, p]
        return total[0], total[1]

    def gather_second(s, k, piece0, piece1):
        ring = 1 - k
        a2s[s, k] = jnp.concatenate([piece0, piece1], axis=0).astype(BF16)
        spread(ring, ag2_(s, k), lambda p: a2s.at[s, k], a2r.at[s, k])

    def gather_first(s, k):
        a2r[s, k, place[1 - k]] = a2s[s, k]
        arrived(a2r.at[s, k, pl.ds(0, 7)], ag2_(s, k))
        both = a2r[s, k].astype(F32)
        zero, one = both[:, :8].reshape(B, CH), both[:, 8:].reshape(B, CH)
        for p in range(N):
            mark = crecv[k, p, 0:1, :]
            a1s[s, k, p] = (zero * (1.0 - mark) + one * mark).astype(BF16)
        spread(k, ag1_(s, k), lambda p: a1s.at[s, k, p], a1r.at[s, k])

    def gathered(s):
        for k in range(2):
            a1r[s, k, place[k]] = a1s[s, k, place[k]]
            arrived(a1r.at[s, k, pl.ds(0, 7)], ag1_(s, k))
            for p in range(N):
                f = chunk_of(k, p)
                wt[:, f * CH:(f + 1) * CH] = a1r[s, k, p]

    def project(quarter):
        rows = slice(quarter * 256, (quarter + 1) * 256)
        return rows, lax.dot_general(wt[...], xbuf[rows, :], (((1,), (1,)), ((), ())), preferred_element_type=F32)

    def upward(rows):
        first = rows.start // TOK
        return jnp.concatenate([rrecv[first].astype(F32), rrecv[first + 1].astype(F32)], axis=1)

    reduce_first(0)
    for k in range(2):
        arrived(crecv.at[k, pl.ds(0, 7)], C_ + k)
    for quarter in range(4):
        rows = slice(quarter * 256, (quarter + 1) * 256)
        curv[:, rows] = forget * upward(rows) * second_slope(prim[:, rows])
    for k in range(2):
        reduce_second(0, k)
    for k in range(2):
        grad0, grad1 = owned(0, k)
        base = wown[k, place[1 - k]]
        gather_second(0, k, base - rate0 * grad0, base - rate1 * grad1)
    for k in range(2):
        gather_first(0, k)
    gathered(0)

    for quarter in range(4):
        rows, value = project(quarter)
        delta[:, rows] = ((1.0 - 2.0 * forget) * upward(rows) * first_slope(value) / LEN).astype(BF16)
    reduce_first(1)
    for k in range(2):
        reduce_second(1, k)
    for k in range(2):
        outer0, outer1 = owned(1, k)
        osum[k] = outer0 + outer1
        gather_second(1, k, outer0, outer1)
    for k in range(2):
        gather_first(1, k)
    gathered(1)

    for quarter in range(4):
        rows, value = project(quarter)
        delta[:, rows] = (curv[:, rows] * value / LEN).astype(BF16)
    reduce_first(2, own_rate)
    for k in range(2):
        arrived(r1.at[2, k, pl.ds(0, 7)], rs1_(2, k))
        own_first(2, k)
        total = r1[2, k, 0].astype(F32)
        for p in range(1, N):
            total = total + r1[2, k, p].astype(F32)
        s2c[k] = total.reshape(8, 8, CH)
        spread(1 - k, rs2_(2, k), lambda p: s2c.at[k, p], r2c.at[k])
    for k in range(2):
        me = place[1 - k]
        r2c[k, me] = s2c[k, me]
        arrived(r2c.at[k, pl.ds(0, 7)], rs2_(2, k))
        total = r2c[k, 0]
        for p in range(1, N):
            total = total + r2c[k, p]
        tile[k] = SCALE * (osum[k] - total)

    spots = (yl, z % 4)
    targets = [spots[k] * 4 + yh * 2 + k for k in range(2)]
    for k in range(2):

        @pl.when(fs != targets[k])
        def _(k=k):
            send(tile.at[k], f1r.at[block], F1_ + k, F1_, (dp, targets[k]))

        @pl.when(fs == targets[k])
        def _(k=k):
            f1r[block] = tile[k]

    @pl.when(c == 0)
    def _():
        @pl.when(x == yl)
        def _():
            arrived(f1r.at[pl.ds(0, 7)], F1_)
            for o in range(1, NYL):
                send(f1r, f2r.at[0], F2_, F2_, (((yl + o) % NYL) * 8 + z, fs))
            f2r[0] = f1r[...]
            gone(f3r.at[pl.ds(0, 3)], F2_)

        @pl.when(x != yl)
        def _():
            arrived(f2r.at[0], F2_)

        def step(o, carry):
            p = (z + o) % N
            send(f2r.at[0], f3r.at[z], F3_, F3_, ring_device(1, p))
            return carry

        lax.fori_loop(1, N, step, 0)
        f3r[z] = f2r[0]

    @pl.when(c == 1)
    def _():
        @pl.when(x == z % 4)
        def _():
            arrived(f1r.at[pl.ds(0, 7)], F1_)

            def step(o, carry):
                p = (z + o) % N
                send(f1r, f2r.at[z // 4], F2_, F2_ + z // 4, ring_device(1, p))
                return carry

            lax.fori_loop(1, N, step, 0)
            f2r[z // 4] = f1r[...]
            arrived(f2r.at[1 - z // 4], F2_ + 1 - z // 4)
            gone(f3r.at[pl.ds(0, 7)], F2_)

        @pl.when(x != z % 4)
        def _():
            arrived(f2r.at[0], F2_)
            arrived(f2r.at[1], F2_ + 1)

        def step(o, carry):
            p = (y + o) % N
            send(f2r.at[p // 4], f3r.at[y], F3_, F3_, ring_device(0, p))
            return carry

        lax.fori_loop(1, N, step, 0)
        f3r[y] = f2r[yh]

    arrived(f3r.at[pl.ds(0, 7)], F3_)
    for pair in range(4):
        both = jnp.concatenate([f3r[:, 2 * pair + i].reshape(B, CH) for i in range(2)], axis=0)
        out_ref[:, pair * 128:(pair + 1) * 128] = both.T

    gone(wrecv.at[pl.ds(0, 15)], W_)
    gone(rrecv.at[pl.ds(0, 7)], R_)
    gone(xbuf.at[pl.ds(0, 14 * (TOK // 2))], X_)
    for k in range(2):
        gone(crecv.at[k, pl.ds(0, 7)], C_ + k)
        for s in range(3):
            gone(r1.at[s, k, pl.ds(0, 7)], rs1_(s, k))
        for s in range(2):
            gone(r2.at[s, k, pl.ds(0, 7)], rs2_(s, k))
            gone(a2r.at[s, k, pl.ds(0, 7)], ag2_(s, k))
            gone(a1r.at[s, k, pl.ds(0, 7)], ag1_(s, k))
        gone(r2c.at[k, pl.ds(0, 7)], rs2_(2, k))

        @pl.when(fs != targets[k])
        def _(k=k):
            gone(tile.at[k], F1_ + k)

    gone(f3r.at[pl.ds(0, 7)], F3_)


def local(tokens, upstream, value_weight, forget_label, copy_index, adv_rate):
    vmem, smem = pl.BlockSpec(memory_space=pltpu.VMEM), pl.BlockSpec(memory_space=pltpu.SMEM)
    return pl.pallas_call(
        kernel,
        out_shape=jax.ShapeDtypeStruct((CH, E), F32),
        in_specs=[pl.BlockSpec(memory_space=pl.ANY), vmem, vmem, smem, smem, smem],
        out_specs=vmem,
        scratch_shapes=[
            pltpu.VMEM((8 * TOK, DW), BF16),
            pltpu.VMEM((8, B, CH), BF16),
            pltpu.VMEM((16, B, CH), BF16),
            pltpu.VMEM((8, B, TOK), BF16),
            pltpu.VMEM((8, B, TOK), BF16),
            pltpu.VMEM((2, 8, 8, 128), F32),
            pltpu.VMEM((B, DW), BF16),
            pltpu.VMEM((2, 8, 8, CH), F32),
            pltpu.VMEM((B, 8 * TOK), F32),
            pltpu.VMEM((B, 8 * TOK), F32),
            pltpu.VMEM((B, 8 * TOK), BF16),
            pltpu.VMEM((3, 2, 8, B, CH), BF16),
            pltpu.VMEM((3, 2, 8, B, CH), BF16),
            pltpu.VMEM((2, 2, 8, 2, 8, CH), F32),
            pltpu.VMEM((2, 2, 8, 2, 8, CH), F32),
            pltpu.VMEM((2, 8, 8, CH), F32),
            pltpu.VMEM((2, 8, 8, CH), F32),
            pltpu.VMEM((2, 2, 16, CH), BF16),
            pltpu.VMEM((2, 2, 8, 16, CH), BF16),
            pltpu.VMEM((2, 2, 8, B, CH), BF16),
            pltpu.VMEM((2, 2, 8, B, CH), BF16),
            pltpu.VMEM((2, 8, CH), F32),
            pltpu.VMEM((2, 8, CH), F32),
            pltpu.VMEM((8, 8, CH), F32),
            pltpu.VMEM((2, 8, 8, CH), F32),
            pltpu.VMEM((8, 8, 8, CH), F32),
            pltpu.SemaphoreType.DMA((GROUPS,)),
            pltpu.SemaphoreType.DMA((GROUPS,)),
            pltpu.SemaphoreType.DMA,
        ],
        compiler_params=pltpu.CompilerParams(collective_id=0, has_side_effects=True, vmem_limit_bytes=48 << 20),
        name="meta_grad",
    )(tokens, upstream, value_weight, forget_label, copy_index, adv_rate)


def solution(mesh):
    in_specs = (
        P(("dp", "fsdp"), None),
        P(("dp", "fsdp"), None),
        P("fsdp", None),
        P("dp"),
        P("dp"),
        P(),
    )
    return jax.shard_map(local, mesh=mesh, in_specs=in_specs, out_specs=P("fsdp", None), check_vma=False)
```

time: 1410 us -> 122 us (0.09); the launches traced: 1380 us -> 122 us
  waiting for transfers between devices: 1320 us -> 0 us
  Pallas kernels: 0 us -> 117 us
  blocking collectives: 17.7 us -> 0 us
  matrix products: 16.4 us -> 0 us
    psum x3 -> x0, waiting for transfers between devices: 858 us -> none  [the longest x1 288 us: local(): stacked = lax.psum(onehot[:, None, None] * grad_local[None], 'dp')]
    all_gather x5 -> x0, waiting for transfers between devices: 360 us -> none  [the longest x1 85.3 us: local(): lax.all_gather(tangent, 'fsdp', axis=0, tiled=True)]
    pallas_call x0 -> x1, Pallas kernels: none -> 117 us  [local(): pl.pallas_call(kernel, out_shape=jax.ShapeDtypeStruct((CH, E), F32), in_s...]
    reduce_scatter x1 -> x0, waiting for transfers between devices: 105 us -> none  [local(): lax.psum_scatter(lax.dot_general(tokens, delta_adv, (((0,), (0,)), ((), (...]
    all_to_all x1 -> x0, blocking collectives: 17.7 us -> none  [local(): lax.all_to_all(tokens, 'fsdp', split_axis=1, concat_axis=0, tiled=True)]
    dot_general x6 -> x0, matrix products: 16.4 us -> none  [the longest x3 7.71 us: project(): return jnp.dot(tokens, piece, preferred_element_type=jnp.float32)]
  transfers between devices with their start and end apart: 9 -> 0, of which waited for: 9 -> 0; matrix products, arithmetic and copies ran while one was open for 0% -> 0% of each run, Pallas kernels for 0% -> 0%
where the time goes in v1:
time: 122 us
  Pallas kernels  117 us (96%)
  local copies, waits for them, and re-layouts  3.55 us (3%)
  between operations  1.34 us (1%)
    pallas_call x1, Pallas kernels, local(): pl.pallas_call(kernel, out_shape=jax.ShapeDtypeStruct((CH, E), F32), in_s...  117 us
    unnamed x9, local copies, waits for them, and re-layouts  3.55 us

profile of v1, /device:TPU:1, one launch (start us, length us, event | category | flops | bytes accessed | tf_op | source)
XLA Modules:
  0.0 122.1 jit_solution(14181441180612873455)
XLA Ops:
  0.7 0.0 copy-start.3
  1.3 0.0 copy-done.3
  1.3 0.0 copy-start
  1.3 1.0 copy-done
  2.4 0.0 copy-start.1
  2.4 0.9 copy-done.1
  3.3 0.0 copy-start.2
  3.3 0.9 copy-done.2
  4.2 117.2 %meta_grad.1 = f32[128,512]{1,0:T(8,128)S(1)} custom-call(bf16[128,2048]{1,0:T(8,128)(2,1)S(1)} %copy-done, bf16[128,512]{1,0:T(8,128)(2,1)S(1)} %copy-done.1, bf16[128,512]{1,0:T(8,128)(2,1)S(1)} %copy-done.2, s32[1]{0:T(128)S(6)} %copy.8.forget_ref, s32[1]{0:T(128)S(6)} %copy.9.copy_ref, f32[2]{0:T(128)S(1)} %copy-done.3), custom_call_target="tpu_custom_call" | custom-call | tf_op jit(solution)/shard_map/meta_grad/pallas_call | solution.py:419
  121.4 0.7 copy.10
Async XLA Ops:
  0.7 0.7 copy-start.3
  1.3 1.0 copy-start
  2.4 0.9 copy-start.1
  3.3 0.9 copy-start.2

commit v2 on v1

--- a/solution.py
+++ b/solution.py
@@ -22,6 +22,7 @@
     return sig * (1.0 - sig) * (2.0 + value * (1.0 - 2.0 * sig))
 
 
+QR = TOK // 4
 W_, R_, C_ = 0, 1, 2
 
 
@@ -41,7 +42,11 @@
     return 20 + 2 * s + k
 
 
-F1_, F2_, F3_, X_, GROUPS = 24, 26, 28, 29, 46
+F1_, F2_, F3_, WY_, X_, GROUPS = 24, 26, 28, 29, 30, 63
+
+
+def far_first(i):
+    return 4 + (2 * (i % 2) - 1) * ((i + 1) // 2)
 
 
 def chunk_of(k, p):
@@ -50,8 +55,8 @@
 
 def kernel(
     tok_ref, up_ref, w_ref, forget_ref, copy_ref, rate_ref, out_ref,
-    xbuf, wsrc, wrecv, rsrc, rrecv, crecv, wt, wown, prim, curv, delta,
-    s1, r1, s2, r2, s2c, r2c, a2s, a2r, a1s, a1r, osum, tile, f1r, f2r, f3r,
+    xbuf, wbuf, ubuf, wsrc, wx, wy, rsrc, rrecv, crecv, wt, wown, prim, curv, delta,
+    s1, r1, s2, r2, s2c, r2c, a2s, a2r, a1s, a1r, osum, tile, f1r, f2s, f2r, f3r,
     ssem, rsem, lsem,
 ):
     dp, fs = lax.axis_index("dp"), lax.axis_index("fsdp")
@@ -68,9 +73,6 @@
     def group_device(dx, dc):
         return (dp, ((x + dx) % NX) * 4 + yh * 2 + (c + dc) % 2)
 
-    def mirror_device(dx, dc):
-        return ((3 - yl) * 8 + z, ((x + dx) % NX) * 4 + (1 - yh) * 2 + (c + dc) % 2)
-
     def send(src, dst, out_group, in_group, device):
         pltpu.make_async_remote_copy(
             src_ref=src, dst_ref=dst, send_sem=ssem.at[out_group], recv_sem=rsem.at[in_group],
@@ -86,21 +88,24 @@
     def spread(ring, group, source, dst):
         me = place[ring]
 
-        def step(o, carry):
-            p = (me + o) % N
+        def step(i, carry):
+            p = (me + far_first(i)) % N
             send(source(p), dst.at[me], group, group, ring_device(ring, p))
             return carry
 
-        lax.fori_loop(1, N, step, 0)
-
-    own = pltpu.make_async_copy(tok_ref, xbuf.at[pl.ds(0, TOK)], lsem)
-    own.start()
+        lax.fori_loop(0, N - 1, step, 0)
+
+    own = [
+        pltpu.make_async_copy(src, dst, lsem.at[i])
+        for i, (src, dst) in enumerate(((w_ref, wbuf), (up_ref, ubuf), (tok_ref, xbuf.at[pl.ds(0, TOK)])))
+    ]
+    for copy_in in own:
+        copy_in.start()
     barrier = pltpu.get_barrier_semaphore()
     for dx in range(NX):
         for dc in range(2):
             if dx or dc:
                 pl.semaphore_signal(barrier, inc=1, device_id=group_device(dx, dc), device_id_type=pl.DeviceIdType.MESH)
-            pl.semaphore_signal(barrier, inc=1, device_id=mirror_device(dx, dc), device_id_type=pl.DeviceIdType.MESH)
     for ring in range(2):
 
         def greet(o, carry, ring=ring):
@@ -110,56 +115,50 @@
 
         lax.fori_loop(1, N, greet, 0)
 
-    wsrc[...] = w_ref[...].T.reshape(8, B, CH)
-    rsrc[...] = up_ref[...].T.reshape(8, B, TOK)
+    own[0].wait()
+    wsrc[...] = wbuf[...].T.reshape(8, 4, 16, CH)
+    own[1].wait()
+    rsrc[...] = ubuf[...].T.reshape(8, B, TOK)
     copy = copy_ref[0].astype(F32)
     forget = forget_ref[0].astype(F32)
     rate0, rate1 = rate_ref[0], rate_ref[1]
     own_rate = rate0 * (1.0 - copy) + rate1 * copy
     crecv[0, y] = jnp.full((8, 128), copy, F32)
     crecv[1, z] = jnp.full((8, 128), copy, F32)
-    own.wait()
-    pl.semaphore_wait(barrier, 29)
+    own[2].wait()
+    pl.semaphore_wait(barrier, 21)
 
     block = 2 * x + c
-    for dx in range(NX):
-        for dc in range(2):
-            to = 2 * ((x + dx) % NX) + (c + dc) % 2
-            if dx or dc:
-                send(wsrc.at[to], wrecv.at[fs], W_, W_, group_device(dx, dc))
-            send(wsrc.at[to], wrecv.at[fs], W_, W_, mirror_device(dx, dc))
-    wrecv[fs] = wsrc[block]
-    for dx in range(NX):
-        for dc in range(2):
-            if dx or dc:
-                to = 2 * ((x + dx) % NX) + (c + dc) % 2
-                send(rsrc.at[to], rrecv.at[2 * (-dx % NX) + dc], R_, R_, group_device(dx, dc))
+    others = [(dx, dc) for dx in range(NX) for dc in range(2) if dx or dc]
+    for dx, dc in others:
+        to = 2 * ((x + dx) % NX) + (c + dc) % 2
+        send(wsrc.at[to, yl], wx.at[block], W_, W_, group_device(dx, dc))
+
+    def part(slot, quarter):
+        return xbuf.at[pl.ds(slot * TOK + quarter * QR, QR)]
+
+    def send_part(from_slot, to_slot, quarter, dx, dc):
+        group = X_ + 1 + 4 * to_slot + quarter
+        send(part(from_slot, quarter), part(to_slot, quarter), X_, group, group_device(dx, dc))
+
+    def part_arrived(slot, quarter):
+        arrived(part(slot, quarter), X_ + 1 + 4 * slot + quarter)
+
+    for i in range(4):
+        send_part(0, 6, i, 1, 0)
+        send_part(0, 2, 3 - i, 3, 0)
+        send_part(0, 1, i, 0, 1)
+    for dx, dc in others:
+        to = 2 * ((x + dx) % NX) + (c + dc) % 2
+        send(rsrc.at[to], rrecv.at[2 * (-dx % NX) + dc], R_, R_, group_device(dx, dc))
     rrecv[0] = rsrc[block]
-
-    def part(slot, half):
-        return xbuf.at[pl.ds(slot * TOK + half * (TOK // 2), TOK // 2)]
-
-    def send_part(from_slot, to_slot, half, dx, dc):
-        send(part(from_slot, half), part(to_slot, half), X_, X_ + 1 + 2 * to_slot + half, group_device(dx, dc))
-
-    def part_arrived(slot, half):
-        arrived(part(slot, half), X_ + 1 + 2 * slot + half)
-
-    send_part(0, 6, 0, 1, 0)
-    send_part(0, 2, 1, 3, 0)
-    send_part(0, 6, 1, 1, 0)
-    send_part(0, 2, 0, 3, 0)
-    send_part(0, 1, 0, 0, 1)
-    send_part(0, 1, 1, 0, 1)
     for ring in range(2):
         spread(ring, C_ + ring, lambda p, ring=ring: crecv.at[ring, place[ring]], crecv.at[ring])
 
-    arrived(wrecv.at[pl.ds(0, 15)], W_)
-    for f in range(16):
-        wt[:, f * CH:(f + 1) * CH] = wrecv[f]
-    for k in range(2):
-        wown[k] = wrecv[chunk_of(k, place[k])].astype(F32).reshape(8, 8, CH)
-    arrived(rrecv.at[pl.ds(0, 7)], R_)
+    wx[block] = wsrc[block, yl]
+    arrived(wx.at[pl.ds(0, 7)], W_)
+    spread(0, WY_, lambda p: wx, wy)
+    wy[y] = wx[...]
 
     def first_pass(slot):
         rows = slice(slot * TOK, (slot + 1) * TOK)
@@ -167,45 +166,58 @@
         prim[:, rows] = value
         delta[:, rows] = (forget * rrecv[slot].astype(F32) * first_slope(value) / LEN).astype(BF16)
 
+    def pass_on(slot, quarter):
+        part_arrived(slot, quarter)
+        send_part(slot, slot + 1, quarter, 0, 1)
+
+    for i in range(2):
+        part_arrived(6, i)
+        send_part(6, 4, i, 1, 0)
+        send_part(6, 7, i, 0, 1)
+        part_arrived(2, 3 - i)
+        send_part(2, 4, 3 - i, 3, 0)
+        send_part(2, 3, 3 - i, 0, 1)
+    for i in range(2):
+        pass_on(6, 2 + i)
+        pass_on(2, 1 - i)
+    arrived(wy.at[pl.ds(0, 7)], WY_)
+    for p in range(N):
+        for b in range(8):
+            f = (b // 2) * 4 + (p // 4) * 2 + b % 2
+            wt[(p % 4) * 16:(p % 4) * 16 + 16, f * CH:(f + 1) * CH] = wy[p, b]
+    for k in range(2):
+        first = pl.multiple_of(chunk_of(k, place[k]) * CH, CH)
+        wown[k] = wt[:, pl.ds(first, CH)].astype(F32).reshape(8, 8, CH)
+    for i in range(4):
+        part_arrived(1, i)
+    arrived(rrecv.at[pl.ds(0, 7)], R_)
     first_pass(0)
-    part_arrived(6, 0)
-    send_part(6, 4, 0, 1, 0)
-    send_part(6, 7, 0, 0, 1)
-    part_arrived(2, 1)
-    send_part(2, 4, 1, 3, 0)
-    send_part(2, 3, 1, 0, 1)
-    part_arrived(1, 0)
-    part_arrived(1, 1)
     first_pass(1)
-    part_arrived(6, 1)
-    send_part(6, 7, 1, 0, 1)
-    part_arrived(2, 0)
-    send_part(2, 3, 0, 0, 1)
+    pass_on(4, 0)
+    pass_on(4, 3)
     first_pass(6)
     first_pass(2)
     for slot in (7, 3):
-        part_arrived(slot, 0)
-        part_arrived(slot, 1)
+        for i in range(4):
+            part_arrived(slot, i)
         first_pass(slot)
-    for half in range(2):
-        part_arrived(4, half)
-        send_part(4, 5, half, 0, 1)
+    pass_on(4, 1)
+    pass_on(4, 2)
     first_pass(4)
-    part_arrived(5, 0)
-    part_arrived(5, 1)
+    for i in range(4):
+        part_arrived(5, i)
     first_pass(5)
 
     def reduce_first(s, factor=None):
         left = delta[...]
 
-        def start(o):
+        def start(i):
             for k in range(2):
-                p = (place[k] + o) % N
+                p = (place[k] + far_first(i)) % N
                 send(s1.at[s, k, p], r1.at[s, k, place[k]], rs1_(s, k), rs1_(s, k), ring_device(k, p))
 
         def step(i, carry):
-            o = i + 1
-            spots = [(place[k] + o) % N for k in range(2)]
+            spots = [(place[k] + far_first(i)) % N for k in range(2)]
             right = jnp.concatenate(
                 [xbuf[:, pl.ds(pl.multiple_of(chunk_of(k, spots[k]) * CH, CH), CH)] for k in range(2)], axis=1)
             sums = jnp.dot(left, right, preferred_element_type=F32)
@@ -213,7 +225,7 @@
                 sums = factor * sums
             for k in range(2):
                 s1[s, k, spots[k]] = sums[:, k * CH:(k + 1) * CH].astype(BF16)
-            pl.when(i > 0)(lambda: start(i))
+            pl.when(i > 0)(lambda: start(i - 1))
             return carry
 
         lax.fori_loop(0, N, step, 0)
@@ -231,18 +243,17 @@
             mark = crecv[k, p, 0:1, :]
             sums[0] = sums[0] + piece * (1.0 - mark)
             sums[1] = sums[1] + piece * mark
-        for copy_at in range(2):
-            s2[s, k, :, copy_at] = sums[copy_at].reshape(8, 8, CH)
+        s2[s, k] = jnp.concatenate([total.reshape(8, 8, CH) for total in sums], axis=1).astype(BF16)
         spread(ring, rs2_(s, k), lambda p: s2.at[s, k, p], r2.at[s, k])
 
     def owned(s, k):
         me = place[1 - k]
         r2[s, k, me] = s2[s, k, me]
         arrived(r2.at[s, k, pl.ds(0, 7)], rs2_(s, k))
-        total = r2[s, k, 0]
+        total = r2[s, k, 0].astype(F32)
         for p in range(1, N):
-            total = total + r2[s, k, p]
-        return total[0], total[1]
+            total = total + r2[s, k, p].astype(F32)
+        return total[:8], total[8:]
 
     def gather_second(s, k, piece0, piece1):
         ring = 1 - k
@@ -343,9 +354,10 @@
         @pl.when(x == yl)
         def _():
             arrived(f1r.at[pl.ds(0, 7)], F1_)
+            f2s[...] = f1r[...].reshape(4, 16, CH).astype(BF16)
             for o in range(1, NYL):
-                send(f1r, f2r.at[0], F2_, F2_, (((yl + o) % NYL) * 8 + z, fs))
-            f2r[0] = f1r[...]
+                send(f2s, f2r.at[0], F2_, F2_, (((yl + o) % NYL) * 8 + z, fs))
+            f2r[0] = f2s[...]
             gone(f3r.at[pl.ds(0, 3)], F2_)
 
         @pl.when(x != yl)
@@ -353,11 +365,11 @@
             arrived(f2r.at[0], F2_)
 
         def step(o, carry):
-            p = (z + o) % N
+            p = (z + far_first(o)) % N
             send(f2r.at[0], f3r.at[z], F3_, F3_, ring_device(1, p))
             return carry
 
-        lax.fori_loop(1, N, step, 0)
+        lax.fori_loop(0, N - 1, step, 0)
         f3r[z] = f2r[0]
 
     @pl.when(c == 1)
@@ -365,14 +377,15 @@
         @pl.when(x == z % 4)
         def _():
             arrived(f1r.at[pl.ds(0, 7)], F1_)
+            f2s[...] = f1r[...].reshape(4, 16, CH).astype(BF16)
 
             def step(o, carry):
-                p = (z + o) % N
-                send(f1r, f2r.at[z // 4], F2_, F2_ + z // 4, ring_device(1, p))
+                p = (z + far_first(o)) % N
+                send(f2s, f2r.at[z // 4], F2_, F2_ + z // 4, ring_device(1, p))
                 return carry
 
-            lax.fori_loop(1, N, step, 0)
-            f2r[z // 4] = f1r[...]
+            lax.fori_loop(0, N - 1, step, 0)
+            f2r[z // 4] = f2s[...]
             arrived(f2r.at[1 - z // 4], F2_ + 1 - z // 4)
             gone(f3r.at[pl.ds(0, 7)], F2_)
 
@@ -382,21 +395,23 @@
             arrived(f2r.at[1], F2_ + 1)
 
         def step(o, carry):
-            p = (y + o) % N
+            p = (y + far_first(o)) % N
             send(f2r.at[p // 4], f3r.at[y], F3_, F3_, ring_device(0, p))
             return carry
 
-        lax.fori_loop(1, N, step, 0)
+        lax.fori_loop(0, N - 1, step, 0)
         f3r[y] = f2r[yh]
 
     arrived(f3r.at[pl.ds(0, 7)], F3_)
+    result = f3r[...].astype(F32).reshape(8, 8, 8, CH)
     for pair in range(4):
-        both = jnp.concatenate([f3r[:, 2 * pair + i].reshape(B, CH) for i in range(2)], axis=0)
+        both = jnp.concatenate([result[:, 2 * pair + i].reshape(B, CH) for i in range(2)], axis=0)
         out_ref[:, pair * 128:(pair + 1) * 128] = both.T
 
-    gone(wrecv.at[pl.ds(0, 15)], W_)
+    gone(wx.at[pl.ds(0, 7)], W_)
+    gone(wy.at[pl.ds(0, 7)], WY_)
     gone(rrecv.at[pl.ds(0, 7)], R_)
-    gone(xbuf.at[pl.ds(0, 14 * (TOK // 2))], X_)
+    gone(xbuf.at[pl.ds(0, 28 * QR)], X_)
     for k in range(2):
         gone(crecv.at[k, pl.ds(0, 7)], C_ + k)
         for s in range(3):
@@ -416,15 +431,19 @@
 
 def local(tokens, upstream, value_weight, forget_label, copy_index, adv_rate):
     vmem, smem = pl.BlockSpec(memory_space=pltpu.VMEM), pl.BlockSpec(memory_space=pltpu.SMEM)
+    hbm = pl.BlockSpec(memory_space=pl.ANY)
     return pl.pallas_call(
         kernel,
         out_shape=jax.ShapeDtypeStruct((CH, E), F32),
-        in_specs=[pl.BlockSpec(memory_space=pl.ANY), vmem, vmem, smem, smem, smem],
+        in_specs=[hbm, hbm, hbm, smem, smem, smem],
         out_specs=vmem,
         scratch_shapes=[
             pltpu.VMEM((8 * TOK, DW), BF16),
-            pltpu.VMEM((8, B, CH), BF16),
-            pltpu.VMEM((16, B, CH), BF16),
+            pltpu.VMEM((CH, E), BF16),
+            pltpu.VMEM((TOK, E), BF16),
+            pltpu.VMEM((8, 4, 16, CH), BF16),
+            pltpu.VMEM((8, 16, CH), BF16),
+            pltpu.VMEM((8, 8, 16, CH), BF16),
             pltpu.VMEM((8, B, TOK), BF16),
             pltpu.VMEM((8, B, TOK), BF16),
             pltpu.VMEM((2, 8, 8, 128), F32),
@@ -435,8 +454,8 @@
             pltpu.VMEM((B, 8 * TOK), BF16),
             pltpu.VMEM((3, 2, 8, B, CH), BF16),
             pltpu.VMEM((3, 2, 8, B, CH), BF16),
-            pltpu.VMEM((2, 2, 8, 2, 8, CH), F32),
-            pltpu.VMEM((2, 2, 8, 2, 8, CH), F32),
+            pltpu.VMEM((2, 2, 8, 16, CH), BF16),
+            pltpu.VMEM((2, 2, 8, 16, CH), BF16),
             pltpu.VMEM((2, 8, 8, CH), F32),
             pltpu.VMEM((2, 8, 8, CH), F32),
             pltpu.VMEM((2, 2, 16, CH), BF16),
@@ -446,13 +465,14 @@
             pltpu.VMEM((2, 8, CH), F32),
             pltpu.VMEM((2, 8, CH), F32),
             pltpu.VMEM((8, 8, CH), F32),
-            pltpu.VMEM((2, 8, 8, CH), F32),
-            pltpu.VMEM((8, 8, 8, CH), F32),
+            pltpu.VMEM((4, 16, CH), BF16),
+            pltpu.VMEM((2, 4, 16, CH), BF16),
+            pltpu.VMEM((8, 4, 16, CH), BF16),
             pltpu.SemaphoreType.DMA((GROUPS,)),
             pltpu.SemaphoreType.DMA((GROUPS,)),
-            pltpu.SemaphoreType.DMA,
+            pltpu.SemaphoreType.DMA((3,)),
         ],
-        compiler_params=pltpu.CompilerParams(collective_id=0, has_side_effects=True, vmem_limit_bytes=48 << 20),
+        compiler_params=pltpu.CompilerParams(collective_id=0, has_side_effects=True, vmem_limit_bytes=(64 << 20) - (400 << 10)),
         name="meta_grad",
     )(tokens, upstream, value_weight, forget_label, copy_index, adv_rate)
 

time: 122 us -> 110 us (0.902)
  Pallas kernels: 117 us -> 106 us
  local copies, waits for them, and re-layouts: 3.55 us -> 1.67 us
    pallas_call x1, Pallas kernels: 117 us -> 106 us  [local(): pl.pallas_call(kernel, out_shape=jax.ShapeDtypeStruct((CH, E), F32), in_s...]
    unnamed x9 -> x1, local copies, waits for them, and re-layouts: 3.55 us -> 1.67 us
where the time goes in v2:
time: 110 us; the launch traced here: 109 us
  Pallas kernels  106 us (96%)
  local copies, waits for them, and re-layouts  1.67 us (2%)
  between operations  1.3 us (1%)
    pallas_call x1, Pallas kernels, local(): pl.pallas_call(kernel, out_shape=jax.ShapeDtypeStruct((CH, E), F32), in_s...  106 us

profile of v2, /device:TPU:1, one launch (start us, length us, event | category | flops | bytes accessed | tf_op | source)
XLA Modules:
  0.0 109.3 jit_solution(11580395242636508575)
XLA Ops:
  1.3 106.4 %meta_grad.1 = f32[128,512]{1,0:T(8,128)} custom-call(bf16[128,2048]{1,0:T(8,128)(2,1)} %tok_ref.1, bf16[128,512]{1,0:T(8,128)(2,1)} %up_ref.1, bf16[128,512]{1,0:T(8,128)(2,1)} %w_ref.1, s32[1]{0:T(128)S(6)} %copy.8.forget_ref, s32[1]{0:T(128)S(6)} %copy.9.copy_ref, f32[2]{0:T(128)} %rate_ref.1), custom_call_target="tpu_custom_call" | custom-call | tf_op jit(solution)/shard_map/meta_grad/pallas_call | solution.py:435
  107.7 1.7 %copy.10 = f32[128,512]{1,0:T(8,128)} copy(f32[128,512]{1,0:T(8,128)} %meta_grad.1) | data formatting | bytes 524288

commit v3 on v2

--- a/solution.py
+++ b/solution.py
@@ -210,25 +210,21 @@
 
     def reduce_first(s, factor=None):
         left = delta[...]
-
-        def start(i):
+        for quarter in range(4):
+            sums = jnp.dot(left, xbuf[:, quarter * 512:(quarter + 1) * 512], preferred_element_type=F32)
+            if factor is not None:
+                sums = factor * sums
+            for i in range(4):
+                f = 4 * quarter + i
+                s1[s, f % 2, f // 4 + 4 * ((f // 2) % 2)] = sums[:, i * CH:(i + 1) * CH].astype(BF16)
+
+        def start(i, carry):
             for k in range(2):
                 p = (place[k] + far_first(i)) % N
                 send(s1.at[s, k, p], r1.at[s, k, place[k]], rs1_(s, k), rs1_(s, k), ring_device(k, p))
-
-        def step(i, carry):
-            spots = [(place[k] + far_first(i)) % N for k in range(2)]
-            right = jnp.concatenate(
-                [xbuf[:, pl.ds(pl.multiple_of(chunk_of(k, spots[k]) * CH, CH), CH)] for k in range(2)], axis=1)
-            sums = jnp.dot(left, right, preferred_element_type=F32)
-            if factor is not None:
-                sums = factor * sums
-            for k in range(2):
-                s1[s, k, spots[k]] = sums[:, k * CH:(k + 1) * CH].astype(BF16)
-            pl.when(i > 0)(lambda: start(i - 1))
             return carry
 
-        lax.fori_loop(0, N, step, 0)
+        lax.fori_loop(0, N - 1, start, 0)
 
     def own_first(s, k):
         r1[s, k, place[k]] = s1[s, k, place[k]]

time: 110 us -> 109 us (level)
  no operation moved by 1% of the time
where the time goes in v3:
time: 109 us
  Pallas kernels  106 us (97%)
  local copies, waits for them, and re-layouts  1.67 us (2%)
  between operations  1.3 us (1%)
    pallas_call x1, Pallas kernels, local(): pl.pallas_call(kernel, out_shape=jax.ShapeDtypeStruct((CH, E), F32), in_s...  106 us

profile of v3, /device:TPU:1, one launch (start us, length us, event | category | flops | bytes accessed | tf_op | source)
XLA Modules:
  0.0 109.1 jit_solution(16427226509100336835)
XLA Ops:
  1.3 106.1 %meta_grad.1 = f32[128,512]{1,0:T(8,128)} custom-call(bf16[128,2048]{1,0:T(8,128)(2,1)} %tok_ref.1, bf16[128,512]{1,0:T(8,128)(2,1)} %up_ref.1, bf16[128,512]{1,0:T(8,128)(2,1)} %w_ref.1, s32[1]{0:T(128)S(6)} %copy.8.forget_ref, s32[1]{0:T(128)S(6)} %copy.9.copy_ref, f32[2]{0:T(128)} %rate_ref.1), custom_call_target="tpu_custom_call" | custom-call | tf_op jit(solution)/shard_map/meta_grad/pallas_call | solution.py:431
  107.4 1.7 %copy.10 = f32[128,512]{1,0:T(8,128)} copy(f32[128,512]{1,0:T(8,128)} %meta_grad.1) | data formatting | bytes 524288
